TPU v7x, 128 devices: a whole 4x4x4 slice. The times are simulated.
128 devices in a mesh: section: 4 (over z), scan: 32 (over x, y, core).
Axes of the slice: x: 4, y: 4, z: 4, core: 2. Of those that a mesh axis runs over, the one named last changes fastest.
Arguments:
- frames: bfloat16 [128, 1024, 2048], P('scan', None, 'section'), may hold values from -6 to 6
- increments: int32 [128], P('scan'), may hold values from 1 to 2
- resample: bfloat16 [256, 32, 32], replicated, may hold values from -1 to 2
- wigner_filter: bfloat16 [2, 128, 1024, 2048], P(None, None, ('section', 'scan')), may hold values from -6 to 6
Outputs:
- deconvolved: bfloat16 [2, 128, 1024, 2048], P(None, None, ('section', 'scan'))
Inputs may be any that keep to these rules, and one draw needn't show every extreme that they name: `increments`: each scan row advances the descan drift by one or two table entries.
All inputs are finite; a program needn't handle non-finite values.
Results may differ from a plain program's by a relative error of at most 0.0066.
Values may be sent and summed in bfloat16 or wider, within the bound.
A program may use at most 192 MiB of HBM per device.

v0:
```python
import math

import jax
import jax.numpy as jnp
from jax.experimental import pallas as pl
from jax.experimental.pallas import tpu as pltpu
from jax import lax
from jax.sharding import PartitionSpec as P

CHUNKS = 2


def fast_matrix(length):
    steps_p = jnp.arange(length, dtype=jnp.int32)
    phase = steps_p[:, None] * steps_p[None, :] % length
    angle = phase.astype(jnp.float32) * (2.0 * math.pi / length)
    return jnp.stack([jnp.cos(angle), -jnp.sin(angle)], axis=0).astype(jnp.bfloat16)


def slow_matrix(row_order, length):
    frequency = jnp.arange(length, dtype=jnp.int32)
    phase = frequency[:, None] * row_order[None, :] % length
    angle = phase.astype(jnp.float32) * (2.0 * math.pi / length)
    cosine = jnp.cos(angle)
    sine = jnp.sin(angle)
    upper = jnp.stack([cosine, sine], axis=1)
    lower = jnp.stack([-sine, cosine], axis=1)
    return jnp.stack([upper, lower], axis=0).astype(jnp.bfloat16)


def slow_kernel(table_ref, *refs, scale, chunks):
    spectrum_refs = refs[:chunks]
    gains_ref, out_ref, gains_wide, out_wide, spectrum_wide = refs[chunks:]
    chunk_q = spectrum_refs[0].shape[0] // table_ref.shape[1]
    q_loc = chunk_q * chunks
    half = gains_ref.shape[1] // q_loc
    depth = table_ref.shape[1]
    table = table_ref[...]
    gains_wide[...] = gains_ref[...].astype(jnp.float32)
    for h in range(chunks):
        spectrum_wide[...] = spectrum_refs[h][...].astype(jnp.float32)
        for k in range(chunk_q):
            q = h * chunk_q + k
            rows = pl.ds(q, half, stride=q_loc)
            columns = spectrum_wide[pl.ds(k, depth, stride=chunk_q), :].astype(jnp.bfloat16)
            grid = jnp.dot(table, columns, preferred_element_type=jnp.float32) * scale
            grid_real = grid[:half]
            grid_imag = grid[half:]
            gain_real = gains_wide[0, rows, :]
            gain_imag = gains_wide[1, rows, :]
            out_wide[0, rows, :] = grid_real * gain_real - grid_imag * gain_imag
            out_wide[1, rows, :] = grid_real * gain_imag + grid_imag * gain_real
    out_ref[...] = out_wide[...].astype(out_ref.dtype)


def slow_and_filter(table, pieces, wigner_filter, scale):
    rows, pixels = pieces[0].shape
    shape = wigner_filter.shape
    flat = wigner_filter.reshape(shape[0], shape[1] * shape[2], shape[3])
    block = 128
    depth = table.shape[1]
    chunks = len(pieces)
    out = pl.pallas_call(
        lambda *refs: slow_kernel(*refs, scale=scale, chunks=chunks),
        grid=(pixels // block,),
        in_specs=[pl.BlockSpec((depth, depth), lambda j: (0, 0))]
        + [pl.BlockSpec((rows, block), lambda j: (0, j))] * chunks
        + [pl.BlockSpec((2, flat.shape[1], block), lambda j: (0, 0, j))],
        out_specs=pl.BlockSpec((2, flat.shape[1], block), lambda j: (0, 0, j)),
        out_shape=jax.ShapeDtypeStruct(flat.shape, jnp.bfloat16),
        scratch_shapes=[pltpu.VMEM((2, flat.shape[1], block), jnp.float32)] * 2
        + [pltpu.VMEM((rows, block), jnp.float32)],
    )(table, *pieces, flat)
    return out.reshape(shape)


def shards(frames, increments, resample, wigner_filter):
    section_count = lax.axis_size("section")
    scan_count = lax.axis_size("scan")
    devices = section_count * scan_count
    rows_loc, positions, pixels_loc = frames.shape
    total_rows = rows_loc * scan_count
    detector_rows = resample.shape[1]
    rows_sec = detector_rows // section_count
    detector_cols = pixels_loc // rows_sec
    q_loc = positions // devices
    chunk_q = q_loc // CHUNKS

    spread = jnp.broadcast_to(increments[None, :], (scan_count, rows_loc))
    every_increment = lax.all_to_all(spread, "scan", 0, 0, tiled=True).reshape(-1)
    shift_index = jnp.cumsum(every_increment) - 1
    matrices = resample[shift_index].reshape(scan_count, rows_loc, detector_rows, section_count, rows_sec)

    steps_p = jnp.arange(positions, dtype=jnp.int32)
    pieces = []
    for h in range(CHUNKS):
        steps_q = (jnp.arange(devices, dtype=jnp.int32)[:, None] * q_loc + h * chunk_q
                   + jnp.arange(chunk_q, dtype=jnp.int32)[None, :])
        phase = steps_q[:, :, None] * steps_p[None, None, :] % positions
        angle = phase.astype(jnp.float32) * (2.0 * math.pi / positions)
        fast_table = jnp.stack([jnp.cos(angle), -jnp.sin(angle)], axis=0).astype(jnp.bfloat16)
        raw = jnp.einsum("cdqp,rpk->dcqrk", fast_table, frames, preferred_element_type=jnp.float32)
        raw = (raw * (1.0 / math.sqrt(positions))).astype(jnp.bfloat16)
        got = lax.all_to_all(raw, ("section", "scan"), 0, 0, tiled=True)
        got = got.reshape(section_count, scan_count, 2, chunk_q, rows_loc, rows_sec, detector_cols)
        spectrum = jnp.einsum("jiasb,sjcqibx->jicqax", matrices, got, preferred_element_type=jnp.float32)
        pieces.append(spectrum.astype(jnp.bfloat16).reshape(total_rows * 2 * chunk_q, detector_rows * detector_cols))
    slow_table = slow_matrix(jnp.arange(total_rows, dtype=jnp.int32), total_rows)
    slow_table = slow_table.transpose(0, 1, 3, 2).reshape(2 * total_rows, 2 * total_rows)
    return slow_and_filter(slow_table, pieces, wigner_filter, 1.0 / math.sqrt(total_rows))


def solution(mesh):
    in_specs = (
        P("scan", None, "section"),
        P("scan"),
        P(),
        P(None, None, ("section", "scan"), None),
    )
    out_specs = P(None, None, ("section", "scan"), None)
    return jax.shard_map(shards, mesh=mesh, in_specs=in_specs, out_specs=out_specs, check_vma=False)
```

profile of v0, /device:TPU:1, one launch (start us, length us, event | category | flops | bytes accessed | tf_op | source)
XLA Modules:
  0.0 205.1 jit_solution(18359390361080914609)
XLA Ops:
  0.0 1.3 broadcast_in_dim.2
  1.3 8.6 %all-to-all-start.1 = ((s32[32,1,4]{2,1,0:T(1,128)}), s32[32,1,4]{2,1,0:T(1,128)S(1)}, u32[]{:S(2)}, u32[]{:S(2)}) async-start(s32[32,1,4]{2,1,0:T(1,128)} %broadcast_in_dim.2), calls=%async_computation.1 | async-start | bytes 32768 | tf_op jit(solution)/shard_map/all_to_all | solution.py:90
  9.9 9.1 %cosine_convert_fusion = (bf16[1,128,4,1024]{3,1,2,0:T(8,128)(2,1)S(1)}, bf16[1,128,4,1024]{3,1,2,0:T(8,128)(2,1)S(1)}) fusion(s32[128,4]{0,1:T(4,128)S(1)} %iota_add_fusion), kind=kLoop, calls=%fused_computation.34 | loop fusion | flops 8912896 | bytes 2099200 | tf_op jit(solution)/shard_map/convert
  18.9 6.9 %fusion.9 = bf16[128,2,4,4,512]{4,0,3,2,1:T(8,128)(2,1)S(1)} fusion(bf16[4,1024,512]{2,1,0:T(8,128)(2,1)} %param.4, bf16[1,128,4,1024]{3,1,2,0:T(8,128)(2,1)S(1)} %get-tuple-element.8, bf16[1,128,4,1024]{3,1,2,0:T(8,128)(2,1)S(1)} %get-tuple-element.7), kind=kOutput, calls=%fused_computation.10 | convolution fusion | flops 4303355904 | bytes 10485760 | tf_op jit(solution)/shard_map/cdqp,rpk->dcqrk/dot_general | solution.py:102
  25.9 5.3 %copy.38 = bf16[128,2,4,4,512]{4,3,2,1,0:T(4,128)(2,1)} copy(bf16[128,2,4,4,512]{4,0,3,2,1:T(8,128)(2,1)S(1)} %fusion.9) | data formatting | bytes 8388608 | tf_op jit(solution)/shard_map/convert_element_type | solution.py:103
  31.1 10.8 %all-to-all-start.2 = ((bf16[128,2,4,4,512]{4,3,2,1,0:T(4,128)(2,1)}), bf16[128,2,4,4,512]{4,3,2,1,0:T(4,128)(2,1)}, u32[]{:S(2)}, u32[]{:S(2)}) async-start(bf16[128,2,4,4,512]{4,3,2,1,0:T(4,128)(2,1)} %copy.38), calls=%async_computation.2 | async-start | bytes 8388608 | tf_op jit(solution)/shard_map/all_to_all | solution.py:104
  41.9 9.1 %cosine_convert_fusion.1 = (bf16[1,128,4,1024]{3,1,2,0:T(8,128)(2,1)S(1)}, bf16[1,128,4,1024]{3,1,2,0:T(8,128)(2,1)S(1)}) fusion(s32[128,4]{0,1:T(4,128)S(1)} %iota_add_fusion.1), kind=kLoop, calls=%fused_computation.38 | loop fusion | flops 8912896 | bytes 2099200 | tf_op jit(solution)/shard_map/convert.2
  51.0 6.9 %fusion.8 = bf16[128,2,4,4,512]{4,0,3,2,1:T(8,128)(2,1)S(1)} fusion(bf16[4,1024,512]{2,1,0:T(8,128)(2,1)} %param.4, bf16[1,128,4,1024]{3,1,2,0:T(8,128)(2,1)S(1)} %get-tuple-element.10, bf16[1,128,4,1024]{3,1,2,0:T(8,128)(2,1)S(1)} %get-tuple-element.9), kind=kOutput, calls=%fused_computation.9 | convolution fusion | flops 4303355904 | bytes 10485760 | tf_op jit(solution)/shard_map/cdqp,rpk->dcqrk/dot_general | solution.py:102
  57.9 5.2 %copy.32 = bf16[128,2,4,4,512]{4,3,2,1,0:T(4,128)(2,1)} copy(bf16[128,2,4,4,512]{4,0,3,2,1:T(8,128)(2,1)S(1)} %fusion.8) | data formatting | bytes 8388608 | tf_op jit(solution)/shard_map/convert_element_type | solution.py:103
  63.1 31.5 %all-to-all-done.2 = bf16[128,2,4,4,512]{4,3,2,1,0:T(4,128)(2,1)} async-done(((bf16[128,2,4,4,512]{4,3,2,1,0:T(4,128)(2,1)}), bf16[128,2,4,4,512]{4,3,2,1,0:T(4,128)(2,1)}, u32[]{:S(2)}, u32[]{:S(2)}) %all-to-all-start.2) | async-done | bytes 4194336 | tf_op jit(solution)/shard_map/all_to_all | solution.py:104
  94.6 5.5 %all-to-all-start = ((bf16[128,2,4,4,512]{4,3,2,1,0:T(4,128)(2,1)}), bf16[128,2,4,4,512]{4,3,2,1,0:T(4,128)(2,1)}, u32[]{:S(2)}, u32[]{:S(2)}) async-start(bf16[128,2,4,4,512]{4,3,2,1,0:T(4,128)(2,1)} %copy.32), calls=%async_computation | async-start | bytes 8388608 | tf_op jit(solution)/shard_map/all_to_all | solution.py:104
  100.9 0.7 copy.41.refs_0_
  101.6 3.0 %copy.35 = bf16[256,32,32]{2,1,0:T(8,128)(2,1)S(1)} copy(bf16[256,32,32]{0,2,1:T(8,128)(2,1)S(1)} %copy-done) | data formatting | bytes 1048576 | tf_op args[2]
  105.1 0.7 reduce.5
  106.2 0.8 gather_fusion
  107.0 0.6 copy.36
  107.6 11.6 %reshape.311 = bf16[4,32,2,4,4,8,64]{6,5,4,3,2,1,0:T(8,128)(2,1)} reshape(bf16[128,2,4,4,512]{4,3,2,1,0:T(4,128)(2,1)} %all-to-all-done.2) | data formatting | bytes 8388608 | tf_op jit(solution)/shard_map/reshape | solution.py:105
  119.2 9.0 %fusion.5 = bf16[32,4,2,4,32,64]{5,4,3,2,1,0:T(8,128)(2,1)} fusion(bf16[32,4,32,4,8,1,1]{2,4,3,6,5,1,0:T(8,128)(2,1)S(1)} %bitcast.65, bf16[4,32,2,4,4,8,64]{6,5,4,3,2,1,0:T(8,128)(2,1)} %reshape.311), kind=kOutput, calls=%fused_computation.8 | convolution fusion | flops 136314880 | bytes 8650752 | tf_op jit(solution)/shard_map/jiasb,sjcqibx->jicqax/dot_general | solution.py:106
  128.2 12.3 %reshape.292.refs_2_ = bf16[1024,2048]{1,0:T(8,128)(2,1)} reshape(bf16[32,4,2,4,32,64]{5,4,3,2,1,0:T(8,128)(2,1)} %fusion.5) | data formatting | bytes 8388608 | tf_op jit(solution)/shard_map/reshape | solution.py:107
  140.5 12.4 %all-to-all-done = bf16[128,2,4,4,512]{4,3,2,1,0:T(4,128)(2,1)} async-done(((bf16[128,2,4,4,512]{4,3,2,1,0:T(4,128)(2,1)}), bf16[128,2,4,4,512]{4,3,2,1,0:T(4,128)(2,1)}, u32[]{:S(2)}, u32[]{:S(2)}) %all-to-all-start) | async-done | bytes 4194336 | tf_op jit(solution)/shard_map/all_to_all | solution.py:104
  152.9 11.6 %reshape.309 = bf16[4,32,2,4,4,8,64]{6,5,4,3,2,1,0:T(8,128)(2,1)} reshape(bf16[128,2,4,4,512]{4,3,2,1,0:T(4,128)(2,1)} %all-to-all-done) | data formatting | bytes 8388608 | tf_op jit(solution)/shard_map/reshape | solution.py:105
  164.6 9.0 %fusion.2 = bf16[32,4,2,4,32,64]{5,4,3,2,1,0:T(8,128)(2,1)} fusion(bf16[32,4,32,4,8,1,1]{2,4,3,6,5,1,0:T(8,128)(2,1)S(1)} %bitcast.66, bf16[4,32,2,4,4,8,64]{6,5,4,3,2,1,0:T(8,128)(2,1)} %reshape.309), kind=kOutput, calls=%fused_computation.7 | convolution fusion | flops 136314880 | bytes 8650752 | tf_op jit(solution)/shard_map/jiasb,sjcqibx->jicqax/dot_general | solution.py:106
  173.6 12.4 %reshape.290.refs_1_ = bf16[1024,2048]{1,0:T(8,128)(2,1)} reshape(bf16[32,4,2,4,32,64]{5,4,3,2,1,0:T(8,128)(2,1)} %fusion.2) | data formatting | bytes 8388608 | tf_op jit(solution)/shard_map/reshape | solution.py:107
  185.9 19.2 %shard_map.46 = bf16[2,1024,2048]{2,1,0:T(8,128)(2,1)} custom-call(bf16[256,256]{1,0:T(8,128)(2,1)} %copy.41.refs_0_, bf16[1024,2048]{1,0:T(8,128)(2,1)} %reshape.290.refs_1_, bf16[1024,2048]{1,0:T(8,128)(2,1)} %reshape.292.refs_2_, bf16[2,1024,2048]{2,1,0:T(8,128)(2,1)} %bitcast.67), custom_call_target="tpu_custom_call" | custom-call | tf_op jit(solution)/shard_map/pallas_call | solution.py:63
  (18 shorter events, 1.6 us)
Async XLA Ops:
  1.3 29.9 %all-to-all-start.1 = ((s32[32,1,4]{2,1,0:T(1,128)}), s32[32,1,4]{2,1,0:T(1,128)S(1)}, u32[]{:S(2)}, u32[]{:S(2)}) async-start(s32[32,1,4]{2,1,0:T(1,128)} %broadcast_in_dim.2), calls=%async_computation.1 | async-start | bytes 32768 | tf_op jit(solution)/shard_map/all_to_all | solution.py:90
  31.1 63.5 %all-to-all-start.2 = ((bf16[128,2,4,4,512]{4,3,2,1,0:T(4,128)(2,1)}), bf16[128,2,4,4,512]{4,3,2,1,0:T(4,128)(2,1)}, u32[]{:S(2)}, u32[]{:S(2)}) async-start(bf16[128,2,4,4,512]{4,3,2,1,0:T(4,128)(2,1)} %copy.38), calls=%async_computation.2 | async-start | bytes 8388608 | tf_op jit(solution)/shard_map/all_to_all | solution.py:104
  63.1 38.5 %copy-start = (bf16[256,32,32]{0,2,1:T(8,128)(2,1)S(1)}, bf16[256,32,32]{0,2,1:T(8,128)(2,1)}, u32[]{:S(2)}) copy-start(bf16[256,32,32]{0,2,1:T(8,128)(2,1)} %param.6) | copy-start | bytes 1572868
  94.6 58.3 %all-to-all-start = ((bf16[128,2,4,4,512]{4,3,2,1,0:T(4,128)(2,1)}), bf16[128,2,4,4,512]{4,3,2,1,0:T(4,128)(2,1)}, u32[]{:S(2)}, u32[]{:S(2)}) async-start(bf16[128,2,4,4,512]{4,3,2,1,0:T(4,128)(2,1)} %copy.32), calls=%async_computation | async-start | bytes 8388608 | tf_op jit(solution)/shard_map/all_to_all | solution.py:104
where the time goes:
time: 207 us; the launch traced here: 205 us
  local copies, waits for them, and re-layouts  65.5 us (32%)
  waiting for transfers between devices  43.9 us (21%)
  matrix products  31.8 us (15%)
  starting transfers between devices  24.8 us (12%)
  other arithmetic  19.7 us (10%)
  Pallas kernels  19.2 us (9%)
    all_to_all x2, waiting for transfers between devices, shards(): got = lax.all_to_all(raw, ('section', 'scan'), 0, 0, tiled=True)  43.9 us
    reshape x2, local copies, waits for them, and re-layouts, shards(): spectrum.astype(jnp.bfloat16)  24.7 us
    reshape x2, local copies, waits for them, and re-layouts, shards(): got.reshape(section_count, scan_count, 2, chunk_q, rows_loc, rows_sec, de...  23.2 us
    pallas_call x1, Pallas kernels, slow_and_filter(): pl.pallas_call(lambda *refs: slow_kernel(*refs, scale=scale, chunks=chunk...  19.2 us
    another operation x5, other arithmetic  18.8 us
    dot_general x2, matrix products, shards(): jnp.einsum('jiasb,sjcqibx->jicqax', matrices, got, preferred_element_type...  18 us
    all_to_all x2, starting transfers between devices, shards(): got = lax.all_to_all(raw, ('section', 'scan'), 0, 0, tiled=True)  16.2 us
    dot_general x2, matrix products, shards(): jnp.einsum('cdqp,rpk->dcqrk', fast_table, frames, preferred_element_type=...  13.8 us
  transfers between devices with their start and end apart: 3, of which 2 were waited for; matrix products, arithmetic and copies ran while one was open for 40% of the time, Pallas kernels for 0%

commit v1 on v0

--- a/solution.py
+++ b/solution.py
@@ -17,6 +17,21 @@
     return jnp.stack([jnp.cos(angle), -jnp.sin(angle)], axis=0).astype(jnp.bfloat16)
 
 
+def fast_rows(steps_q, length):
+    low = 32
+    steps_low = jnp.arange(low, dtype=jnp.int32)
+    steps_high = jnp.arange(length // low, dtype=jnp.int32) * low
+    scale = 2.0 * math.pi / length
+    angle_high = (steps_q[..., None] * steps_high % length).astype(jnp.float32) * scale
+    angle_low = (steps_q[..., None] * steps_low % length).astype(jnp.float32) * scale
+    cos_high, sin_high = jnp.cos(angle_high)[..., :, None], jnp.sin(angle_high)[..., :, None]
+    cos_low, sin_low = jnp.cos(angle_low)[..., None, :], jnp.sin(angle_low)[..., None, :]
+    cosine = cos_high * cos_low - sin_high * sin_low
+    sine = sin_high * cos_low + cos_high * sin_low
+    table = jnp.stack([cosine, -sine], axis=0)
+    return table.reshape(table.shape[:-2] + (length,)).astype(jnp.bfloat16)
+
+
 def slow_matrix(row_order, length):
     frequency = jnp.arange(length, dtype=jnp.int32)
     phase = frequency[:, None] * row_order[None, :] % length
@@ -30,24 +45,22 @@
 
 def slow_kernel(table_ref, *refs, scale, chunks):
     spectrum_refs = refs[:chunks]
-    gains_ref, out_ref, gains_wide, out_wide, spectrum_wide = refs[chunks:]
+    gains_ref, out_ref, out_wide = refs[chunks:]
     chunk_q = spectrum_refs[0].shape[0] // table_ref.shape[1]
     q_loc = chunk_q * chunks
     half = gains_ref.shape[1] // q_loc
     depth = table_ref.shape[1]
     table = table_ref[...]
-    gains_wide[...] = gains_ref[...].astype(jnp.float32)
     for h in range(chunks):
-        spectrum_wide[...] = spectrum_refs[h][...].astype(jnp.float32)
         for k in range(chunk_q):
             q = h * chunk_q + k
             rows = pl.ds(q, half, stride=q_loc)
-            columns = spectrum_wide[pl.ds(k, depth, stride=chunk_q), :].astype(jnp.bfloat16)
+            columns = spectrum_refs[h][pl.ds(k, depth, stride=chunk_q), :]
             grid = jnp.dot(table, columns, preferred_element_type=jnp.float32) * scale
             grid_real = grid[:half]
             grid_imag = grid[half:]
-            gain_real = gains_wide[0, rows, :]
-            gain_imag = gains_wide[1, rows, :]
+            gain_real = gains_ref[0, rows, :].astype(jnp.float32)
+            gain_imag = gains_ref[1, rows, :].astype(jnp.float32)
             out_wide[0, rows, :] = grid_real * gain_real - grid_imag * gain_imag
             out_wide[1, rows, :] = grid_real * gain_imag + grid_imag * gain_real
     out_ref[...] = out_wide[...].astype(out_ref.dtype)
@@ -68,8 +81,7 @@
         + [pl.BlockSpec((2, flat.shape[1], block), lambda j: (0, 0, j))],
         out_specs=pl.BlockSpec((2, flat.shape[1], block), lambda j: (0, 0, j)),
         out_shape=jax.ShapeDtypeStruct(flat.shape, jnp.bfloat16),
-        scratch_shapes=[pltpu.VMEM((2, flat.shape[1], block), jnp.float32)] * 2
-        + [pltpu.VMEM((rows, block), jnp.float32)],
+        scratch_shapes=[pltpu.VMEM((2, flat.shape[1], block), jnp.float32)],
     )(table, *pieces, flat)
     return out.reshape(shape)
 
@@ -91,14 +103,11 @@
     shift_index = jnp.cumsum(every_increment) - 1
     matrices = resample[shift_index].reshape(scan_count, rows_loc, detector_rows, section_count, rows_sec)
 
-    steps_p = jnp.arange(positions, dtype=jnp.int32)
     pieces = []
     for h in range(CHUNKS):
         steps_q = (jnp.arange(devices, dtype=jnp.int32)[:, None] * q_loc + h * chunk_q
                    + jnp.arange(chunk_q, dtype=jnp.int32)[None, :])
-        phase = steps_q[:, :, None] * steps_p[None, None, :] % positions
-        angle = phase.astype(jnp.float32) * (2.0 * math.pi / positions)
-        fast_table = jnp.stack([jnp.cos(angle), -jnp.sin(angle)], axis=0).astype(jnp.bfloat16)
+        fast_table = fast_rows(steps_q, positions)
         raw = jnp.einsum("cdqp,rpk->dcqrk", fast_table, frames, preferred_element_type=jnp.float32)
         raw = (raw * (1.0 / math.sqrt(positions))).astype(jnp.bfloat16)
         got = lax.all_to_all(raw, ("section", "scan"), 0, 0, tiled=True)

time: 207 us -> 204 us (0.986)
  other arithmetic: 19.7 us -> 4.95 us
  waiting for transfers between devices: 43.9 us -> 51.9 us
  local copies, waits for them, and re-layouts: 65.5 us -> 70.1 us
    another operation x5 -> x4, other arithmetic: 18.8 us -> 3.05 us
    all_to_all x2, waiting for transfers between devices: 43.9 us -> 51.9 us  [shards(): got = lax.all_to_all(raw, ('section', 'scan'), 0, 0, tiled=True)]
    sub x0 -> x2, local copies, waits for them, and re-layouts: none -> 2.8 us  [fast_rows(): cosine = cos_high * cos_low - sin_high * sin_low]
  transfers between devices with their start and end apart: 3 -> 3, of which waited for: 2 -> 2; matrix products, arithmetic and copies ran while one was open for 40% -> 36% of each run, Pallas kernels for 0% -> 0%
where the time goes in v1:
time: 204 us; the launch traced here: 202 us
  local copies, waits for them, and re-layouts  70.1 us (34%)
  waiting for transfers between devices  51.9 us (25%)
  matrix products  32.2 us (16%)
  starting transfers between devices  24.8 us (12%)
  Pallas kernels  17.9 us (9%)
  other arithmetic  4.95 us (2%)
    all_to_all x2, waiting for transfers between devices, shards(): got = lax.all_to_all(raw, ('section', 'scan'), 0, 0, tiled=True)  51.9 us
    reshape x2, local copies, waits for them, and re-layouts, shards(): spectrum.astype(jnp.bfloat16)  24.7 us
    reshape x2, local copies, waits for them, and re-layouts, shards(): got.reshape(section_count, scan_count, 2, chunk_q, rows_loc, rows_sec, de...  23.2 us
    dot_general x2, matrix products, shards(): jnp.einsum('jiasb,sjcqibx->jicqax', matrices, got, preferred_element_type...  18 us
    pallas_call x1, Pallas kernels, slow_and_filter(): pl.pallas_call(lambda *refs: slow_kernel(*refs, scale=scale, chunks=chunk...  17.9 us
    all_to_all x2, starting transfers between devices, shards(): got = lax.all_to_all(raw, ('section', 'scan'), 0, 0, tiled=True)  16.3 us
    dot_general x2, matrix products, shards(): jnp.einsum('cdqp,rpk->dcqrk', fast_table, frames, preferred_element_type=...  14.2 us
    convert_element_type x2, local copies, waits for them, and re-layouts, shards(): raw = (raw * (1.0 / math.sqrt(positions))).astype(jnp.bfloat16)  10.4 us
  transfers between devices with their start and end apart: 3, of which 2 were waited for; matrix products, arithmetic and copies ran while one was open for 36% of the time, Pallas kernels for 0%

profile of v1, /device:TPU:1, one launch (start us, length us, event | category | flops | bytes accessed | tf_op | source)
XLA Modules:
  0.0 202.1 jit_solution(1117621682896499495)
XLA Ops:
  0.0 1.3 broadcast_in_dim.2
  1.3 8.6 %all-to-all-start.1 = ((s32[32,1,4]{2,1,0:T(1,128)}), s32[32,1,4]{2,1,0:T(1,128)S(1)}, u32[]{:S(2)}, u32[]{:S(2)}) async-start(s32[32,1,4]{2,1,0:T(1,128)} %broadcast_in_dim.2), calls=%async_computation.1 | async-start | bytes 32768 | tf_op jit(solution)/shard_map/all_to_all | solution.py:102
  9.9 1.1 fusion.50
  11.0 2.3 %subtract_convert_fusion = (bf16[128,4,32,32]{0,3,2,1:T(8,128)(2,1)}, bf16[128,4,32,32]{0,3,2,1:T(8,128)(2,1)S(1)}, bf16[128,4,32,32]{0,3,2,1:T(8,128)(2,1)S(1)}, bf16[128,4,32,32]{0,3,2,1:T(8,128)(2,1)S(1)}) fusion(f32[128,4,32]{0,2,1:T(8,128)S(1)} %get-tuple-element.15, f32[128,4,32]{0,2,1:T(8,128)S(1)} %get-tuple-element.12, ...), kind=kLoop, calls=%fused_computation.22 | loop fusion | flops 9437184 | bytes 4718592 | tf_op jit(solution)/shard_map/convert.3
  13.3 2.3 %copy.52 = bf16[1,128,4,1024]{3,1,2,0:T(8,128)(2,1)} copy(bf16[1,128,4,1024]{1,3,2,0:T(8,128)(2,1)} %bitcast.75) | data formatting | bytes 2097152 | tf_op jit(solution)/shard_map/sub | solution.py:29
  15.6 1.3 copy.53
  16.9 7.3 %fusion.9 = bf16[128,2,4,4,512]{4,0,3,2,1:T(8,128)(2,1)S(1)} fusion(bf16[4,1024,512]{2,1,0:T(8,128)(2,1)} %param.4, bf16[1,128,4,1024]{3,1,2,0:T(8,128)(2,1)} %copy.53, bf16[1,128,4,1024]{3,1,2,0:T(8,128)(2,1)} %copy.52), kind=kOutput, calls=%fused_computation.10 | convolution fusion | flops 4303355904 | bytes 10485760 | tf_op jit(solution)/shard_map/cdqp,rpk->dcqrk/dot_general | solution.py:111
  24.2 5.3 %copy.54 = bf16[128,2,4,4,512]{4,3,2,1,0:T(4,128)(2,1)} copy(bf16[128,2,4,4,512]{4,0,3,2,1:T(8,128)(2,1)S(1)} %fusion.9) | data formatting | bytes 8388608 | tf_op jit(solution)/shard_map/convert_element_type | solution.py:112
  29.4 10.8 %all-to-all-start.2 = ((bf16[128,2,4,4,512]{4,3,2,1,0:T(4,128)(2,1)}), bf16[128,2,4,4,512]{4,3,2,1,0:T(4,128)(2,1)}, u32[]{:S(2)}, u32[]{:S(2)}) async-start(bf16[128,2,4,4,512]{4,3,2,1,0:T(4,128)(2,1)} %copy.54), calls=%async_computation.2 | async-start | bytes 8388608 | tf_op jit(solution)/shard_map/all_to_all | solution.py:113
  41.3 6.9 %fusion.8 = bf16[128,2,4,4,512]{4,0,3,2,1:T(8,128)(2,1)S(1)} fusion(bf16[4,1024,512]{2,1,0:T(8,128)(2,1)} %param.4, bf16[1,128,4,1024]{3,1,2,0:T(8,128)(2,1)S(1)} %copy.45, bf16[1,128,4,1024]{3,1,2,0:T(8,128)(2,1)S(1)} %copy.44), kind=kOutput, calls=%fused_computation.9 | convolution fusion | flops 4303355904 | bytes 10485760 | tf_op jit(solution)/shard_map/cdqp,rpk->dcqrk/dot_general | solution.py:111
  48.2 5.2 %copy.46 = bf16[128,2,4,4,512]{4,3,2,1,0:T(4,128)(2,1)} copy(bf16[128,2,4,4,512]{4,0,3,2,1:T(8,128)(2,1)S(1)} %fusion.8) | data formatting | bytes 8388608 | tf_op jit(solution)/shard_map/convert_element_type | solution.py:112
  53.4 39.5 %all-to-all-done.2 = bf16[128,2,4,4,512]{4,3,2,1,0:T(4,128)(2,1)} async-done(((bf16[128,2,4,4,512]{4,3,2,1,0:T(4,128)(2,1)}), bf16[128,2,4,4,512]{4,3,2,1,0:T(4,128)(2,1)}, u32[]{:S(2)}, u32[]{:S(2)}) %all-to-all-start.2) | async-done | bytes 4194336 | tf_op jit(solution)/shard_map/all_to_all | solution.py:113
  92.9 5.5 %all-to-all-start = ((bf16[128,2,4,4,512]{4,3,2,1,0:T(4,128)(2,1)}), bf16[128,2,4,4,512]{4,3,2,1,0:T(4,128)(2,1)}, u32[]{:S(2)}, u32[]{:S(2)}) async-start(bf16[128,2,4,4,512]{4,3,2,1,0:T(4,128)(2,1)} %copy.46), calls=%async_computation | async-start | bytes 8388608 | tf_op jit(solution)/shard_map/all_to_all | solution.py:113
  98.4 3.0 %copy.49 = bf16[256,32,32]{2,1,0:T(8,128)(2,1)S(1)} copy(bf16[256,32,32]{0,2,1:T(8,128)(2,1)S(1)} %copy-done) | data formatting | bytes 1048576 | tf_op args[2]
  102.2 0.7 copy.57.refs_0_
  104.5 0.8 gather_fusion
  105.9 11.6 %reshape.487 = bf16[4,32,2,4,4,8,64]{6,5,4,3,2,1,0:T(8,128)(2,1)} reshape(bf16[128,2,4,4,512]{4,3,2,1,0:T(4,128)(2,1)} %all-to-all-done.2) | data formatting | bytes 8388608 | tf_op jit(solution)/shard_map/reshape | solution.py:114
  117.6 9.0 %fusion.5 = bf16[32,4,2,4,32,64]{5,4,3,2,1,0:T(8,128)(2,1)} fusion(bf16[32,4,32,4,8,1,1]{2,4,3,6,5,1,0:T(8,128)(2,1)S(1)} %bitcast.69, bf16[4,32,2,4,4,8,64]{6,5,4,3,2,1,0:T(8,128)(2,1)} %reshape.487), kind=kOutput, calls=%fused_computation.8 | convolution fusion | flops 136314880 | bytes 8650752 | tf_op jit(solution)/shard_map/jiasb,sjcqibx->jicqax/dot_general | solution.py:115
  126.5 12.3 %reshape.468.refs_2_ = bf16[1024,2048]{1,0:T(8,128)(2,1)} reshape(bf16[32,4,2,4,32,64]{5,4,3,2,1,0:T(8,128)(2,1)} %fusion.5) | data formatting | bytes 8388608 | tf_op jit(solution)/shard_map/reshape | solution.py:116
  138.9 12.4 %all-to-all-done = bf16[128,2,4,4,512]{4,3,2,1,0:T(4,128)(2,1)} async-done(((bf16[128,2,4,4,512]{4,3,2,1,0:T(4,128)(2,1)}), bf16[128,2,4,4,512]{4,3,2,1,0:T(4,128)(2,1)}, u32[]{:S(2)}, u32[]{:S(2)}) %all-to-all-start) | async-done | bytes 4194336 | tf_op jit(solution)/shard_map/all_to_all | solution.py:113
  151.3 11.6 %reshape.485 = bf16[4,32,2,4,4,8,64]{6,5,4,3,2,1,0:T(8,128)(2,1)} reshape(bf16[128,2,4,4,512]{4,3,2,1,0:T(4,128)(2,1)} %all-to-all-done) | data formatting | bytes 8388608 | tf_op jit(solution)/shard_map/reshape | solution.py:114
  162.9 9.0 %fusion.2 = bf16[32,4,2,4,32,64]{5,4,3,2,1,0:T(8,128)(2,1)} fusion(bf16[32,4,32,4,8,1,1]{2,4,3,6,5,1,0:T(8,128)(2,1)S(1)} %bitcast.70, bf16[4,32,2,4,4,8,64]{6,5,4,3,2,1,0:T(8,128)(2,1)} %reshape.485), kind=kOutput, calls=%fused_computation.7 | convolution fusion | flops 136314880 | bytes 8650752 | tf_op jit(solution)/shard_map/jiasb,sjcqibx->jicqax/dot_general | solution.py:115
  171.9 12.4 %reshape.466.refs_1_ = bf16[1024,2048]{1,0:T(8,128)(2,1)} reshape(bf16[32,4,2,4,32,64]{5,4,3,2,1,0:T(8,128)(2,1)} %fusion.2) | data formatting | bytes 8388608 | tf_op jit(solution)/shard_map/reshape | solution.py:116
  184.2 17.9 %shard_map.46 = bf16[2,1024,2048]{2,1,0:T(8,128)(2,1)} custom-call(bf16[256,256]{1,0:T(8,128)(2,1)} %copy.57.refs_0_, bf16[1024,2048]{1,0:T(8,128)(2,1)} %reshape.466.refs_1_, bf16[1024,2048]{1,0:T(8,128)(2,1)} %reshape.468.refs_2_, bf16[2,1024,2048]{2,1,0:T(8,128)(2,1)} %bitcast.71), custom_call_target="tpu_custom_call" | custom-call | tf_op jit(solution)/shard_map/pallas_call | solution.py:76
  (23 shorter events, 4.0 us)
Async XLA Ops:
  1.3 28.2 %all-to-all-start.1 = ((s32[32,1,4]{2,1,0:T(1,128)}), s32[32,1,4]{2,1,0:T(1,128)S(1)}, u32[]{:S(2)}, u32[]{:S(2)}) async-start(s32[32,1,4]{2,1,0:T(1,128)} %broadcast_in_dim.2), calls=%async_computation.1 | async-start | bytes 32768 | tf_op jit(solution)/shard_map/all_to_all | solution.py:102
  29.4 63.5 %all-to-all-start.2 = ((bf16[128,2,4,4,512]{4,3,2,1,0:T(4,128)(2,1)}), bf16[128,2,4,4,512]{4,3,2,1,0:T(4,128)(2,1)}, u32[]{:S(2)}, u32[]{:S(2)}) async-start(bf16[128,2,4,4,512]{4,3,2,1,0:T(4,128)(2,1)} %copy.54), calls=%async_computation.2 | async-start | bytes 8388608 | tf_op jit(solution)/shard_map/all_to_all | solution.py:113
  53.4 45.0 %copy-start = (bf16[256,32,32]{0,2,1:T(8,128)(2,1)S(1)}, bf16[256,32,32]{0,2,1:T(8,128)(2,1)}, u32[]{:S(2)}) copy-start(bf16[256,32,32]{0,2,1:T(8,128)(2,1)} %param.6) | copy-start | bytes 1572868
  92.9 58.3 %all-to-all-start = ((bf16[128,2,4,4,512]{4,3,2,1,0:T(4,128)(2,1)}), bf16[128,2,4,4,512]{4,3,2,1,0:T(4,128)(2,1)}, u32[]{:S(2)}, u32[]{:S(2)}) async-start(bf16[128,2,4,4,512]{4,3,2,1,0:T(4,128)(2,1)} %copy.46), calls=%async_computation | async-start | bytes 8388608 | tf_op jit(solution)/shard_map/all_to_all | solution.py:113

commit v2 on v1

--- a/solution.py
+++ b/solution.py
@@ -7,7 +7,7 @@
 from jax import lax
 from jax.sharding import PartitionSpec as P
 
-CHUNKS = 2
+CHUNK_SIZES = (1, 1)
 
 
 def fast_matrix(length):
@@ -43,19 +43,19 @@
     return jnp.stack([upper, lower], axis=0).astype(jnp.bfloat16)
 
 
-def slow_kernel(table_ref, *refs, scale, chunks):
+def slow_kernel(table_ref, *refs, scale, sizes):
+    chunks = len(sizes)
     spectrum_refs = refs[:chunks]
     gains_ref, out_ref, out_wide = refs[chunks:]
-    chunk_q = spectrum_refs[0].shape[0] // table_ref.shape[1]
-    q_loc = chunk_q * chunks
+    q_loc = sum(sizes)
     half = gains_ref.shape[1] // q_loc
     depth = table_ref.shape[1]
     table = table_ref[...]
     for h in range(chunks):
-        for k in range(chunk_q):
-            q = h * chunk_q + k
+        for k in range(sizes[h]):
+            q = sum(sizes[:h]) + k
             rows = pl.ds(q, half, stride=q_loc)
-            columns = spectrum_refs[h][pl.ds(k, depth, stride=chunk_q), :]
+            columns = spectrum_refs[h][pl.ds(k, depth, stride=sizes[h]), :]
             grid = jnp.dot(table, columns, preferred_element_type=jnp.float32) * scale
             grid_real = grid[:half]
             grid_imag = grid[half:]
@@ -67,17 +67,17 @@
 
 
 def slow_and_filter(table, pieces, wigner_filter, scale):
-    rows, pixels = pieces[0].shape
+    pixels = pieces[0].shape[1]
     shape = wigner_filter.shape
     flat = wigner_filter.reshape(shape[0], shape[1] * shape[2], shape[3])
     block = 128
     depth = table.shape[1]
-    chunks = len(pieces)
+    sizes = tuple(piece.shape[0] // depth for piece in pieces)
     out = pl.pallas_call(
-        lambda *refs: slow_kernel(*refs, scale=scale, chunks=chunks),
+        lambda *refs: slow_kernel(*refs, scale=scale, sizes=sizes),
         grid=(pixels // block,),
         in_specs=[pl.BlockSpec((depth, depth), lambda j: (0, 0))]
-        + [pl.BlockSpec((rows, block), lambda j: (0, j))] * chunks
+        + [pl.BlockSpec((piece.shape[0], block), lambda j: (0, j)) for piece in pieces]
         + [pl.BlockSpec((2, flat.shape[1], block), lambda j: (0, 0, j))],
         out_specs=pl.BlockSpec((2, flat.shape[1], block), lambda j: (0, 0, j)),
         out_shape=jax.ShapeDtypeStruct(flat.shape, jnp.bfloat16),
@@ -96,24 +96,26 @@
     rows_sec = detector_rows // section_count
     detector_cols = pixels_loc // rows_sec
     q_loc = positions // devices
-    chunk_q = q_loc // CHUNKS
-
-    spread = jnp.broadcast_to(increments[None, :], (scan_count, rows_loc))
-    every_increment = lax.all_to_all(spread, "scan", 0, 0, tiled=True).reshape(-1)
-    shift_index = jnp.cumsum(every_increment) - 1
-    matrices = resample[shift_index].reshape(scan_count, rows_loc, detector_rows, section_count, rows_sec)
+    sizes = tuple(q_loc * size // sum(CHUNK_SIZES) for size in CHUNK_SIZES)
 
     pieces = []
-    for h in range(CHUNKS):
-        steps_q = (jnp.arange(devices, dtype=jnp.int32)[:, None] * q_loc + h * chunk_q
+    for h, chunk_q in enumerate(sizes):
+        steps_q = (jnp.arange(devices, dtype=jnp.int32)[:, None] * q_loc + sum(sizes[:h])
                    + jnp.arange(chunk_q, dtype=jnp.int32)[None, :])
         fast_table = fast_rows(steps_q, positions)
+        if h == 1:
+            fast_table, increments = lax.optimization_barrier((fast_table, increments))
+            spread = jnp.broadcast_to(increments[None, :], (scan_count, rows_loc))
+            every_increment = lax.all_to_all(spread, "scan", 0, 0, tiled=True).reshape(-1)
+            shift_index = jnp.cumsum(every_increment) - 1
+            matrices = resample[shift_index].reshape(scan_count, rows_loc, detector_rows, section_count, rows_sec)
         raw = jnp.einsum("cdqp,rpk->dcqrk", fast_table, frames, preferred_element_type=jnp.float32)
         raw = (raw * (1.0 / math.sqrt(positions))).astype(jnp.bfloat16)
         got = lax.all_to_all(raw, ("section", "scan"), 0, 0, tiled=True)
-        got = got.reshape(section_count, scan_count, 2, chunk_q, rows_loc, rows_sec, detector_cols)
-        spectrum = jnp.einsum("jiasb,sjcqibx->jicqax", matrices, got, preferred_element_type=jnp.float32)
-        pieces.append(spectrum.astype(jnp.bfloat16).reshape(total_rows * 2 * chunk_q, detector_rows * detector_cols))
+        pieces.append(got.reshape(section_count, scan_count, 2, chunk_q, rows_loc, rows_sec, detector_cols))
+    for h, chunk_q in enumerate(sizes):
+        spectrum = jnp.einsum("jiasb,sjcqibx->jicqax", matrices, pieces[h], preferred_element_type=jnp.float32)
+        pieces[h] = spectrum.astype(jnp.bfloat16).reshape(total_rows * 2 * chunk_q, detector_rows * detector_cols)
     slow_table = slow_matrix(jnp.arange(total_rows, dtype=jnp.int32), total_rows)
     slow_table = slow_table.transpose(0, 1, 3, 2).reshape(2 * total_rows, 2 * total_rows)
     return slow_and_filter(slow_table, pieces, wigner_filter, 1.0 / math.sqrt(total_rows))

time: 204 us -> 200 us (0.980)
  local copies, waits for them, and re-layouts: 70.1 us -> 65.9 us
    sub x2 -> x1, local copies, waits for them, and re-layouts: 2.8 us -> 0.53 us  [fast_rows(): cosine = cos_high * cos_low - sin_high * sin_low]
  transfers between devices with their start and end apart: 3 -> 3, of which waited for: 2 -> 2; matrix products, arithmetic and copies ran while one was open for 36% -> 33% of each run, Pallas kernels for 0% -> 0%
where the time goes in v2:
time: 200 us; the launch traced here: 198 us
  local copies, waits for them, and re-layouts  65.9 us (33%)
  waiting for transfers between devices  51.9 us (26%)
  matrix products  32.2 us (16%)
  starting transfers between devices  24.8 us (12%)
  Pallas kernels  17.9 us (9%)
  other arithmetic  5.35 us (3%)
    all_to_all x2, waiting for transfers between devices, shards(): got = lax.all_to_all(raw, ('section', 'scan'), 0, 0, tiled=True)  51.9 us
    reshape x2, local copies, waits for them, and re-layouts, shards(): spectrum.astype(jnp.bfloat16)  24.7 us
    reshape x2, local copies, waits for them, and re-layouts, shards(): got.reshape(section_count, scan_count, 2, chunk_q, rows_loc, rows_sec, de...  23.2 us
    dot_general x2, matrix products, shards(): jnp.einsum('jiasb,sjcqibx->jicqax', matrices, pieces[h], preferred_elemen...  18 us
    pallas_call x1, Pallas kernels, slow_and_filter(): pl.pallas_call(lambda *refs: slow_kernel(*refs, scale=scale, sizes=sizes)...  17.9 us
    all_to_all x2, starting transfers between devices, shards(): got = lax.all_to_all(raw, ('section', 'scan'), 0, 0, tiled=True)  16.2 us
    dot_general x2, matrix products, shards(): jnp.einsum('cdqp,rpk->dcqrk', fast_table, frames, preferred_element_type=...  14.3 us
    convert_element_type x2, local copies, waits for them, and re-layouts, shards(): raw = (raw * (1.0 / math.sqrt(positions))).astype(jnp.bfloat16)  10.4 us
  transfers between devices with their start and end apart: 3, of which 2 were waited for; matrix products, arithmetic and copies ran while one was open for 33% of the time, Pallas kernels for 0%

profile of v2, /device:TPU:1, one launch (start us, length us, event | category | flops | bytes accessed | tf_op | source)
XLA Modules:
  0.0 198.4 jit_solution(8782414831254499948)
XLA Ops:
  0.0 1.1 fusion.53
  1.1 1.2 subtract_convert_fusion
  2.4 1.5 pad_maximum_fusion
  4.5 8.6 %all-to-all-start.1 = ((s32[32,1,4]{2,1,0:T(1,128)}), s32[32,1,4]{2,1,0:T(1,128)S(1)}, u32[]{:S(2)}, u32[]{:S(2)}) async-start(s32[32,1,4]{2,1,0:T(1,128)} %broadcast_in_dim.2), calls=%async_computation.1 | async-start | bytes 32768 | tf_op jit(solution)/shard_map/all_to_all | solution.py:109
  13.1 7.4 %fusion.9 = bf16[128,2,4,4,512]{4,0,3,2,1:T(8,128)(2,1)S(1)} fusion(bf16[4,1024,512]{2,1,0:T(8,128)(2,1)} %param.4, bf16[2,128,4,1024]{1,3,2,0:T(8,128)(2,1)} %pad_maximum_fusion), kind=kOutput, calls=%fused_computation.10 | convolution fusion | flops 4299161600 | bytes 10485760 | tf_op jit(solution)/shard_map/cdqp,rpk->dcqrk/dot_general | solution.py:112
  20.4 5.3 %copy.50 = bf16[128,2,4,4,512]{4,3,2,1,0:T(4,128)(2,1)} copy(bf16[128,2,4,4,512]{4,0,3,2,1:T(8,128)(2,1)S(1)} %fusion.9) | data formatting | bytes 8388608 | tf_op jit(solution)/shard_map/convert_element_type | solution.py:113
  25.7 10.8 %all-to-all-start.2 = ((bf16[128,2,4,4,512]{4,3,2,1,0:T(4,128)(2,1)}), bf16[128,2,4,4,512]{4,3,2,1,0:T(4,128)(2,1)}, u32[]{:S(2)}, u32[]{:S(2)}) async-start(bf16[128,2,4,4,512]{4,3,2,1,0:T(4,128)(2,1)} %copy.50), calls=%async_computation.2 | async-start | bytes 8388608 | tf_op jit(solution)/shard_map/all_to_all | solution.py:114
  37.5 6.9 %fusion.8 = bf16[128,2,4,4,512]{4,0,3,2,1:T(8,128)(2,1)S(1)} fusion(bf16[4,1024,512]{2,1,0:T(8,128)(2,1)} %param.4, bf16[1,128,4,1024]{3,1,2,0:T(8,128)(2,1)S(1)} %copy.42, bf16[1,128,4,1024]{3,1,2,0:T(8,128)(2,1)S(1)} %copy.41), kind=kOutput, calls=%fused_computation.9 | convolution fusion | flops 4303355904 | bytes 10485760 | tf_op jit(solution)/shard_map/cdqp,rpk->dcqrk/dot_general | solution.py:112
  44.5 5.2 %copy.43 = bf16[128,2,4,4,512]{4,3,2,1,0:T(4,128)(2,1)} copy(bf16[128,2,4,4,512]{4,0,3,2,1:T(8,128)(2,1)S(1)} %fusion.8) | data formatting | bytes 8388608 | tf_op jit(solution)/shard_map/convert_element_type | solution.py:113
  49.6 39.5 %all-to-all-done.2 = bf16[128,2,4,4,512]{4,3,2,1,0:T(4,128)(2,1)} async-done(((bf16[128,2,4,4,512]{4,3,2,1,0:T(4,128)(2,1)}), bf16[128,2,4,4,512]{4,3,2,1,0:T(4,128)(2,1)}, u32[]{:S(2)}, u32[]{:S(2)}) %all-to-all-start.2) | async-done | bytes 4194336 | tf_op jit(solution)/shard_map/all_to_all | solution.py:114
  89.2 5.5 %all-to-all-start = ((bf16[128,2,4,4,512]{4,3,2,1,0:T(4,128)(2,1)}), bf16[128,2,4,4,512]{4,3,2,1,0:T(4,128)(2,1)}, u32[]{:S(2)}, u32[]{:S(2)}) async-start(bf16[128,2,4,4,512]{4,3,2,1,0:T(4,128)(2,1)} %copy.43), calls=%async_computation | async-start | bytes 8388608 | tf_op jit(solution)/shard_map/all_to_all | solution.py:114
  94.7 3.0 %copy.46 = bf16[256,32,32]{2,1,0:T(8,128)(2,1)S(1)} copy(bf16[256,32,32]{0,2,1:T(8,128)(2,1)S(1)} %copy-done) | data formatting | bytes 1048576 | tf_op args[2]
  98.4 0.7 copy.53.refs_0_
  99.7 0.7 reduce.5
  100.8 0.8 gather_fusion
  101.5 0.6 copy.47
  102.2 11.6 %reshape.487 = bf16[4,32,2,4,4,8,64]{6,5,4,3,2,1,0:T(8,128)(2,1)} reshape(bf16[128,2,4,4,512]{4,3,2,1,0:T(4,128)(2,1)} %all-to-all-done.2) | data formatting | bytes 8388608 | tf_op jit(solution)/shard_map/reshape | solution.py:115
  113.8 9.0 %fusion.5 = bf16[32,4,2,4,32,64]{5,4,3,2,1,0:T(8,128)(2,1)} fusion(bf16[32,4,32,4,8,1,1]{2,4,3,6,5,1,0:T(8,128)(2,1)S(1)} %bitcast.69, bf16[4,32,2,4,4,8,64]{6,5,4,3,2,1,0:T(8,128)(2,1)} %reshape.487), kind=kOutput, calls=%fused_computation.8 | convolution fusion | flops 136314880 | bytes 8650752 | tf_op jit(solution)/shard_map/jiasb,sjcqibx->jicqax/dot_general | solution.py:117
  122.8 12.3 %reshape.468.refs_2_ = bf16[1024,2048]{1,0:T(8,128)(2,1)} reshape(bf16[32,4,2,4,32,64]{5,4,3,2,1,0:T(8,128)(2,1)} %fusion.5) | data formatting | bytes 8388608 | tf_op jit(solution)/shard_map/reshape | solution.py:118
  135.1 12.4 %all-to-all-done = bf16[128,2,4,4,512]{4,3,2,1,0:T(4,128)(2,1)} async-done(((bf16[128,2,4,4,512]{4,3,2,1,0:T(4,128)(2,1)}), bf16[128,2,4,4,512]{4,3,2,1,0:T(4,128)(2,1)}, u32[]{:S(2)}, u32[]{:S(2)}) %all-to-all-start) | async-done | bytes 4194336 | tf_op jit(solution)/shard_map/all_to_all | solution.py:114
  147.5 11.6 %reshape.485 = bf16[4,32,2,4,4,8,64]{6,5,4,3,2,1,0:T(8,128)(2,1)} reshape(bf16[128,2,4,4,512]{4,3,2,1,0:T(4,128)(2,1)} %all-to-all-done) | data formatting | bytes 8388608 | tf_op jit(solution)/shard_map/reshape | solution.py:115
  159.1 9.0 %fusion.2 = bf16[32,4,2,4,32,64]{5,4,3,2,1,0:T(8,128)(2,1)} fusion(bf16[32,4,32,4,8,1,1]{2,4,3,6,5,1,0:T(8,128)(2,1)S(1)} %bitcast.70, bf16[4,32,2,4,4,8,64]{6,5,4,3,2,1,0:T(8,128)(2,1)} %reshape.485), kind=kOutput, calls=%fused_computation.7 | convolution fusion | flops 136314880 | bytes 8650752 | tf_op jit(solution)/shard_map/jiasb,sjcqibx->jicqax/dot_general | solution.py:117
  168.1 12.4 %reshape.466.refs_1_ = bf16[1024,2048]{1,0:T(8,128)(2,1)} reshape(bf16[32,4,2,4,32,64]{5,4,3,2,1,0:T(8,128)(2,1)} %fusion.2) | data formatting | bytes 8388608 | tf_op jit(solution)/shard_map/reshape | solution.py:118
  180.5 17.9 %shard_map.46 = bf16[2,1024,2048]{2,1,0:T(8,128)(2,1)} custom-call(bf16[256,256]{1,0:T(8,128)(2,1)} %copy.53.refs_0_, bf16[1024,2048]{1,0:T(8,128)(2,1)} %reshape.466.refs_1_, bf16[1024,2048]{1,0:T(8,128)(2,1)} %reshape.468.refs_2_, bf16[2,1024,2048]{2,1,0:T(8,128)(2,1)} %bitcast.71), custom_call_target="tpu_custom_call" | custom-call | tf_op jit(solution)/shard_map/pallas_call | solution.py:76
  (24 shorter events, 3.3 us)
Async XLA Ops:
  1.1 2.8 %copy-start.1 = (s32[4]{0:T(128)S(1)}, s32[4]{0:T(128)}, u32[]{:S(2)}) copy-start(s32[4]{0:T(128)} %param.5) | copy-start | bytes 52
  4.5 21.2 %all-to-all-start.1 = ((s32[32,1,4]{2,1,0:T(1,128)}), s32[32,1,4]{2,1,0:T(1,128)S(1)}, u32[]{:S(2)}, u32[]{:S(2)}) async-start(s32[32,1,4]{2,1,0:T(1,128)} %broadcast_in_dim.2), calls=%async_computation.1 | async-start | bytes 32768 | tf_op jit(solution)/shard_map/all_to_all | solution.py:109
  25.7 63.5 %all-to-all-start.2 = ((bf16[128,2,4,4,512]{4,3,2,1,0:T(4,128)(2,1)}), bf16[128,2,4,4,512]{4,3,2,1,0:T(4,128)(2,1)}, u32[]{:S(2)}, u32[]{:S(2)}) async-start(bf16[128,2,4,4,512]{4,3,2,1,0:T(4,128)(2,1)} %copy.50), calls=%async_computation.2 | async-start | bytes 8388608 | tf_op jit(solution)/shard_map/all_to_all | solution.py:114
  49.6 45.0 %copy-start = (bf16[256,32,32]{0,2,1:T(8,128)(2,1)S(1)}, bf16[256,32,32]{0,2,1:T(8,128)(2,1)}, u32[]{:S(2)}) copy-start(bf16[256,32,32]{0,2,1:T(8,128)(2,1)} %param.6) | copy-start | bytes 1572868
  89.2 58.3 %all-to-all-start = ((bf16[128,2,4,4,512]{4,3,2,1,0:T(4,128)(2,1)}), bf16[128,2,4,4,512]{4,3,2,1,0:T(4,128)(2,1)}, u32[]{:S(2)}, u32[]{:S(2)}) async-start(bf16[128,2,4,4,512]{4,3,2,1,0:T(4,128)(2,1)} %copy.43), calls=%async_computation | async-start | bytes 8388608 | tf_op jit(solution)/shard_map/all_to_all | solution.py:114

commit v3 on v2

--- a/solution.py
+++ b/solution.py
@@ -48,7 +48,7 @@
     spectrum_refs = refs[:chunks]
     gains_ref, out_ref, out_wide = refs[chunks:]
     q_loc = sum(sizes)
-    half = gains_ref.shape[1] // q_loc
+    half = gains_ref.shape[2]
     depth = table_ref.shape[1]
     table = table_ref[...]
     for h in range(chunks):
@@ -59,8 +59,8 @@
             grid = jnp.dot(table, columns, preferred_element_type=jnp.float32) * scale
             grid_real = grid[:half]
             grid_imag = grid[half:]
-            gain_real = gains_ref[0, rows, :].astype(jnp.float32)
-            gain_imag = gains_ref[1, rows, :].astype(jnp.float32)
+            gain_real = gains_ref[0, q].astype(jnp.float32)
+            gain_imag = gains_ref[1, q].astype(jnp.float32)
             out_wide[0, rows, :] = grid_real * gain_real - grid_imag * gain_imag
             out_wide[1, rows, :] = grid_real * gain_imag + grid_imag * gain_real
     out_ref[...] = out_wide[...].astype(out_ref.dtype)
@@ -70,6 +70,7 @@
     pixels = pieces[0].shape[1]
     shape = wigner_filter.shape
     flat = wigner_filter.reshape(shape[0], shape[1] * shape[2], shape[3])
+    gains = wigner_filter.transpose(0, 2, 1, 3)
     block = 128
     depth = table.shape[1]
     sizes = tuple(piece.shape[0] // depth for piece in pieces)
@@ -78,11 +79,11 @@
         grid=(pixels // block,),
         in_specs=[pl.BlockSpec((depth, depth), lambda j: (0, 0))]
         + [pl.BlockSpec((piece.shape[0], block), lambda j: (0, j)) for piece in pieces]
-        + [pl.BlockSpec((2, flat.shape[1], block), lambda j: (0, 0, j))],
+        + [pl.BlockSpec((2, shape[2], shape[1], block), lambda j: (0, 0, 0, j))],
         out_specs=pl.BlockSpec((2, flat.shape[1], block), lambda j: (0, 0, j)),
         out_shape=jax.ShapeDtypeStruct(flat.shape, jnp.bfloat16),
         scratch_shapes=[pltpu.VMEM((2, flat.shape[1], block), jnp.float32)],
-    )(table, *pieces, flat)
+    )(table, *pieces, gains)
     return out.reshape(shape)
 
 

time: 200 us -> 200 us (level)
  local copies, waits for them, and re-layouts: 65.9 us -> 77.2 us
  waiting for transfers between devices: 51.9 us -> 40.7 us
    all_to_all x2, waiting for transfers between devices: 51.9 us -> 40.7 us  [shards(): got = lax.all_to_all(raw, ('section', 'scan'), 0, 0, tiled=True)]
    unnamed x6 -> x7, local copies, waits for them, and re-layouts: 3.03 us -> 14.3 us
  transfers between devices with their start and end apart: 3 -> 3, of which waited for: 2 -> 2; matrix products, arithmetic and copies ran while one was open for 33% -> 39% of each run, Pallas kernels for 0% -> 0%
where the time goes in v3:
time: 200 us; the launch traced here: 198 us
  local copies, waits for them, and re-layouts  77.2 us (39%)
  waiting for transfers between devices  40.7 us (20%)
  matrix products  32.3 us (16%)
  starting transfers between devices  24.8 us (12%)
  Pallas kernels  17.7 us (9%)
  other arithmetic  5.35 us (3%)
    all_to_all x2, waiting for transfers between devices, shards(): got = lax.all_to_all(raw, ('section', 'scan'), 0, 0, tiled=True)  40.7 us
    reshape x2, local copies, waits for them, and re-layouts, shards(): spectrum.astype(jnp.bfloat16)  24.7 us
    reshape x2, local copies, waits for them, and re-layouts, shards(): got.reshape(section_count, scan_count, 2, chunk_q, rows_loc, rows_sec, de...  23.3 us
    dot_general x2, matrix products, shards(): jnp.einsum('jiasb,sjcqibx->jicqax', matrices, pieces[h], preferred_elemen...  18 us
    pallas_call x1, Pallas kernels, slow_and_filter(): pl.pallas_call(lambda *refs: slow_kernel(*refs, scale=scale, sizes=sizes)...  17.7 us
    all_to_all x2, starting transfers between devices, shards(): got = lax.all_to_all(raw, ('section', 'scan'), 0, 0, tiled=True)  16.2 us
    dot_general x2, matrix products, shards(): jnp.einsum('cdqp,rpk->dcqrk', fast_table, frames, preferred_element_type=...  14.3 us
    unnamed x7, local copies, waits for them, and re-layouts  14.3 us
  transfers between devices with their start and end apart: 3, of which 2 were waited for; matrix products, arithmetic and copies ran while one was open for 39% of the time, Pallas kernels for 0%

profile of v3, /device:TPU:1, one launch (start us, length us, event | category | flops | bytes accessed | tf_op | source)
XLA Modules:
  0.0 198.2 jit_solution(13015125482184856561)
XLA Ops:
  0.0 1.1 fusion.53
  1.1 1.2 subtract_convert_fusion
  2.4 1.5 pad_maximum_fusion
  4.5 8.6 %all-to-all-start.1 = ((s32[32,1,4]{2,1,0:T(1,128)}), s32[32,1,4]{2,1,0:T(1,128)S(1)}, u32[]{:S(2)}, u32[]{:S(2)}) async-start(s32[32,1,4]{2,1,0:T(1,128)} %broadcast_in_dim.2), calls=%async_computation.1 | async-start | bytes 32768 | tf_op jit(solution)/shard_map/all_to_all | solution.py:110
  13.1 7.4 %fusion.9 = bf16[128,2,4,4,512]{4,0,3,2,1:T(8,128)(2,1)S(1)} fusion(bf16[4,1024,512]{2,1,0:T(8,128)(2,1)} %param.4, bf16[2,128,4,1024]{1,3,2,0:T(8,128)(2,1)} %pad_maximum_fusion), kind=kOutput, calls=%fused_computation.11 | convolution fusion | flops 4299161600 | bytes 10485760 | tf_op jit(solution)/shard_map/cdqp,rpk->dcqrk/dot_general | solution.py:113
  20.4 5.3 %copy.54 = bf16[128,2,4,4,512]{4,3,2,1,0:T(4,128)(2,1)} copy(bf16[128,2,4,4,512]{4,0,3,2,1:T(8,128)(2,1)S(1)} %fusion.9) | data formatting | bytes 8388608 | tf_op jit(solution)/shard_map/convert_element_type | solution.py:114
  25.7 10.8 %all-to-all-start.2 = ((bf16[128,2,4,4,512]{4,3,2,1,0:T(4,128)(2,1)}), bf16[128,2,4,4,512]{4,3,2,1,0:T(4,128)(2,1)}, u32[]{:S(2)}, u32[]{:S(2)}) async-start(bf16[128,2,4,4,512]{4,3,2,1,0:T(4,128)(2,1)} %copy.54), calls=%async_computation.2 | async-start | bytes 8388608 | tf_op jit(solution)/shard_map/all_to_all | solution.py:115
  37.5 6.9 %fusion.8 = bf16[128,2,4,4,512]{4,0,3,2,1:T(8,128)(2,1)S(1)} fusion(bf16[4,1024,512]{2,1,0:T(8,128)(2,1)} %param.4, bf16[1,128,4,1024]{3,1,2,0:T(8,128)(2,1)S(1)} %copy.46, bf16[1,128,4,1024]{3,1,2,0:T(8,128)(2,1)S(1)} %copy.45), kind=kOutput, calls=%fused_computation.10 | convolution fusion | flops 4303355904 | bytes 10485760 | tf_op jit(solution)/shard_map/cdqp,rpk->dcqrk/dot_general | solution.py:113
  44.5 5.2 %copy.47 = bf16[128,2,4,4,512]{4,3,2,1,0:T(4,128)(2,1)} copy(bf16[128,2,4,4,512]{4,0,3,2,1:T(8,128)(2,1)S(1)} %fusion.8) | data formatting | bytes 8388608 | tf_op jit(solution)/shard_map/convert_element_type | solution.py:114
  49.6 39.5 %all-to-all-done.2 = bf16[128,2,4,4,512]{4,3,2,1,0:T(4,128)(2,1)} async-done(((bf16[128,2,4,4,512]{4,3,2,1,0:T(4,128)(2,1)}), bf16[128,2,4,4,512]{4,3,2,1,0:T(4,128)(2,1)}, u32[]{:S(2)}, u32[]{:S(2)}) %all-to-all-start.2) | async-done | bytes 4194336 | tf_op jit(solution)/shard_map/all_to_all | solution.py:115
  89.2 5.5 %all-to-all-start = ((bf16[128,2,4,4,512]{4,3,2,1,0:T(4,128)(2,1)}), bf16[128,2,4,4,512]{4,3,2,1,0:T(4,128)(2,1)}, u32[]{:S(2)}, u32[]{:S(2)}) async-start(bf16[128,2,4,4,512]{4,3,2,1,0:T(4,128)(2,1)} %copy.47), calls=%async_computation | async-start | bytes 8388608 | tf_op jit(solution)/shard_map/all_to_all | solution.py:115
  95.4 0.8 copy.58.refs_0_
  96.2 3.0 %copy.50 = bf16[256,32,32]{2,1,0:T(8,128)(2,1)S(1)} copy(bf16[256,32,32]{0,2,1:T(8,128)(2,1)S(1)} %copy-done) | data formatting | bytes 1048576 | tf_op args[2]
  99.2 11.2 %copy.82 = bf16[2,128,8,2048]{3,1,2,0:T(8,128)(2,1)} copy(bf16[2,128,8,2048]{3,2,1,0:T(8,128)(2,1)} %param.7) | data formatting | bytes 16777216 | tf_op args[3]
  110.9 0.7 reduce.5
  112.0 0.8 gather_fusion
  113.4 11.6 %reshape.483 = bf16[4,32,2,4,4,8,64]{6,5,4,3,2,1,0:T(8,128)(2,1)} reshape(bf16[128,2,4,4,512]{4,3,2,1,0:T(4,128)(2,1)} %all-to-all-done.2) | data formatting | bytes 8388608 | tf_op jit(solution)/shard_map/reshape | solution.py:116
  125.0 9.0 %fusion.5 = bf16[32,4,2,4,32,64]{5,4,3,2,1,0:T(8,128)(2,1)} fusion(bf16[32,4,32,4,8,1,1]{2,4,3,6,5,1,0:T(8,128)(2,1)S(1)} %bitcast.72, bf16[4,32,2,4,4,8,64]{6,5,4,3,2,1,0:T(8,128)(2,1)} %reshape.483), kind=kOutput, calls=%fused_computation.9 | convolution fusion | flops 136314880 | bytes 8650752 | tf_op jit(solution)/shard_map/jiasb,sjcqibx->jicqax/dot_general | solution.py:118
  134.0 12.3 %reshape.465.refs_2_ = bf16[1024,2048]{1,0:T(8,128)(2,1)} reshape(bf16[32,4,2,4,32,64]{5,4,3,2,1,0:T(8,128)(2,1)} %fusion.5) | data formatting | bytes 8388608 | tf_op jit(solution)/shard_map/reshape | solution.py:119
  146.3 1.2 all-to-all-done
  147.5 11.6 %reshape.481 = bf16[4,32,2,4,4,8,64]{6,5,4,3,2,1,0:T(8,128)(2,1)} reshape(bf16[128,2,4,4,512]{4,3,2,1,0:T(4,128)(2,1)} %all-to-all-done) | data formatting | bytes 8388608 | tf_op jit(solution)/shard_map/reshape | solution.py:116
  159.1 9.0 %fusion.2 = bf16[32,4,2,4,32,64]{5,4,3,2,1,0:T(8,128)(2,1)} fusion(bf16[32,4,32,4,8,1,1]{2,4,3,6,5,1,0:T(8,128)(2,1)S(1)} %bitcast.73, bf16[4,32,2,4,4,8,64]{6,5,4,3,2,1,0:T(8,128)(2,1)} %reshape.481), kind=kOutput, calls=%fused_computation.8 | convolution fusion | flops 136314880 | bytes 8650752 | tf_op jit(solution)/shard_map/jiasb,sjcqibx->jicqax/dot_general | solution.py:118
  168.1 12.4 %reshape.463.refs_1_ = bf16[1024,2048]{1,0:T(8,128)(2,1)} reshape(bf16[32,4,2,4,32,64]{5,4,3,2,1,0:T(8,128)(2,1)} %fusion.2) | data formatting | bytes 8388608 | tf_op jit(solution)/shard_map/reshape | solution.py:119
  180.5 17.7 %shard_map.46 = bf16[2,1024,2048]{2,1,0:T(8,128)(2,1)} custom-call(bf16[256,256]{1,0:T(8,128)(2,1)} %copy.58.refs_0_, bf16[1024,2048]{1,0:T(8,128)(2,1)} %reshape.463.refs_1_, bf16[1024,2048]{1,0:T(8,128)(2,1)} %reshape.465.refs_2_, bf16[2,8,128,2048]{3,2,1,0:T(8,128)(2,1)} %bitcast.71), custom_call_target="tpu_custom_call" | custom-call | tf_op jit(solution)/shard_map/pallas_call | solution.py:77
  (25 shorter events, 3.9 us)
Async XLA Ops:
  1.1 2.8 %copy-start.1 = (s32[4]{0:T(128)S(1)}, s32[4]{0:T(128)}, u32[]{:S(2)}) copy-start(s32[4]{0:T(128)} %param.5) | copy-start | bytes 52
  4.5 21.2 %all-to-all-start.1 = ((s32[32,1,4]{2,1,0:T(1,128)}), s32[32,1,4]{2,1,0:T(1,128)S(1)}, u32[]{:S(2)}, u32[]{:S(2)}) async-start(s32[32,1,4]{2,1,0:T(1,128)} %broadcast_in_dim.2), calls=%async_computation.1 | async-start | bytes 32768 | tf_op jit(solution)/shard_map/all_to_all | solution.py:110
  25.7 63.5 %all-to-all-start.2 = ((bf16[128,2,4,4,512]{4,3,2,1,0:T(4,128)(2,1)}), bf16[128,2,4,4,512]{4,3,2,1,0:T(4,128)(2,1)}, u32[]{:S(2)}, u32[]{:S(2)}) async-start(bf16[128,2,4,4,512]{4,3,2,1,0:T(4,128)(2,1)} %copy.54), calls=%async_computation.2 | async-start | bytes 8388608 | tf_op jit(solution)/shard_map/all_to_all | solution.py:115
  49.6 46.5 %copy-start = (bf16[256,32,32]{0,2,1:T(8,128)(2,1)S(1)}, bf16[256,32,32]{0,2,1:T(8,128)(2,1)}, u32[]{:S(2)}) copy-start(bf16[256,32,32]{0,2,1:T(8,128)(2,1)} %param.6) | copy-start | bytes 1572868
  89.2 58.3 %all-to-all-start = ((bf16[128,2,4,4,512]{4,3,2,1,0:T(4,128)(2,1)}), bf16[128,2,4,4,512]{4,3,2,1,0:T(4,128)(2,1)}, u32[]{:S(2)}, u32[]{:S(2)}) async-start(bf16[128,2,4,4,512]{4,3,2,1,0:T(4,128)(2,1)} %copy.47), calls=%async_computation | async-start | bytes 8388608 | tf_op jit(solution)/shard_map/all_to_all | solution.py:115

commit v4 on v3

--- a/solution.py
+++ b/solution.py
@@ -46,24 +46,26 @@
 def slow_kernel(table_ref, *refs, scale, sizes):
     chunks = len(sizes)
     spectrum_refs = refs[:chunks]
-    gains_ref, out_ref, out_wide = refs[chunks:]
-    q_loc = sum(sizes)
+    gains_ref, out_ref = refs[chunks:]
     half = gains_ref.shape[2]
     depth = table_ref.shape[1]
     table = table_ref[...]
+    real_parts = []
+    imag_parts = []
     for h in range(chunks):
         for k in range(sizes[h]):
             q = sum(sizes[:h]) + k
-            rows = pl.ds(q, half, stride=q_loc)
             columns = spectrum_refs[h][pl.ds(k, depth, stride=sizes[h]), :]
             grid = jnp.dot(table, columns, preferred_element_type=jnp.float32) * scale
             grid_real = grid[:half]
             grid_imag = grid[half:]
             gain_real = gains_ref[0, q].astype(jnp.float32)
             gain_imag = gains_ref[1, q].astype(jnp.float32)
-            out_wide[0, rows, :] = grid_real * gain_real - grid_imag * gain_imag
-            out_wide[1, rows, :] = grid_real * gain_imag + grid_imag * gain_real
-    out_ref[...] = out_wide[...].astype(out_ref.dtype)
+            real_parts.append(grid_real * gain_real - grid_imag * gain_imag)
+            imag_parts.append(grid_real * gain_imag + grid_imag * gain_real)
+    width = out_ref.shape[2]
+    out_ref[0] = jnp.stack(real_parts, axis=1).reshape(-1, width).astype(out_ref.dtype)
+    out_ref[1] = jnp.stack(imag_parts, axis=1).reshape(-1, width).astype(out_ref.dtype)
 
 
 def slow_and_filter(table, pieces, wigner_filter, scale):
@@ -82,7 +84,6 @@
         + [pl.BlockSpec((2, shape[2], shape[1], block), lambda j: (0, 0, 0, j))],
         out_specs=pl.BlockSpec((2, flat.shape[1], block), lambda j: (0, 0, j)),
         out_shape=jax.ShapeDtypeStruct(flat.shape, jnp.bfloat16),
-        scratch_shapes=[pltpu.VMEM((2, flat.shape[1], block), jnp.float32)],
     )(table, *pieces, gains)
     return out.reshape(shape)
 

time: 200 us -> 208 us (1.040)
  Pallas kernels: 17.7 us -> 25.3 us
    pallas_call x1, Pallas kernels: 17.7 us -> 25.3 us  [slow_and_filter(): pl.pallas_call(lambda *refs: slow_kernel(*refs, scale=scale, sizes=sizes)...]
  transfers between devices with their start and end apart: 3 -> 3, of which waited for: 2 -> 2; matrix products, arithmetic and copies ran while one was open for 39% -> 38% of each run, Pallas kernels for 0% -> 0%
where the time goes in v4:
time: 208 us; the launch traced here: 206 us
  local copies, waits for them, and re-layouts  77.2 us (37%)
  waiting for transfers between devices  40.7 us (20%)
  matrix products  32.3 us (16%)
  Pallas kernels  25.3 us (12%)
  starting transfers between devices  24.8 us (12%)
  other arithmetic  5.35 us (3%)
    all_to_all x2, waiting for transfers between devices, shards(): got = lax.all_to_all(raw, ('section', 'scan'), 0, 0, tiled=True)  40.7 us
    pallas_call x1, Pallas kernels, slow_and_filter(): pl.pallas_call(lambda *refs: slow_kernel(*refs, scale=scale, sizes=sizes)...  25.3 us
    reshape x2, local copies, waits for them, and re-layouts, shards(): spectrum.astype(jnp.bfloat16)  24.7 us
    reshape x2, local copies, waits for them, and re-layouts, shards(): got.reshape(section_count, scan_count, 2, chunk_q, rows_loc, rows_sec, de...  23.3 us
    dot_general x2, matrix products, shards(): jnp.einsum('jiasb,sjcqibx->jicqax', matrices, pieces[h], preferred_elemen...  18 us
    all_to_all x2, starting transfers between devices, shards(): got = lax.all_to_all(raw, ('section', 'scan'), 0, 0, tiled=True)  16.2 us
    dot_general x2, matrix products, shards(): jnp.einsum('cdqp,rpk->dcqrk', fast_table, frames, preferred_element_type=...  14.3 us
    unnamed x7, local copies, waits for them, and re-layouts  14.3 us
  transfers between devices with their start and end apart: 3, of which 2 were waited for; matrix products, arithmetic and copies ran while one was open for 38% of the time, Pallas kernels for 0%

profile of v4, /device:TPU:1, one launch (start us, length us, event | category | flops | bytes accessed | tf_op | source)
XLA Modules:
  0.0 205.8 jit_solution(3208623043953658473)
XLA Ops:
  0.0 1.1 fusion.53
  1.1 1.2 subtract_convert_fusion
  2.4 1.5 pad_maximum_fusion
  4.5 8.6 %all-to-all-start.1 = ((s32[32,1,4]{2,1,0:T(1,128)}), s32[32,1,4]{2,1,0:T(1,128)S(1)}, u32[]{:S(2)}, u32[]{:S(2)}) async-start(s32[32,1,4]{2,1,0:T(1,128)} %broadcast_in_dim.2), calls=%async_computation.1 | async-start | bytes 32768 | tf_op jit(solution)/shard_map/all_to_all | solution.py:111
  13.1 7.4 %fusion.9 = bf16[128,2,4,4,512]{4,0,3,2,1:T(8,128)(2,1)S(1)} fusion(bf16[4,1024,512]{2,1,0:T(8,128)(2,1)} %param.4, bf16[2,128,4,1024]{1,3,2,0:T(8,128)(2,1)} %pad_maximum_fusion), kind=kOutput, calls=%fused_computation.11 | convolution fusion | flops 4299161600 | bytes 10485760 | tf_op jit(solution)/shard_map/cdqp,rpk->dcqrk/dot_general | solution.py:114
  20.4 5.3 %copy.54 = bf16[128,2,4,4,512]{4,3,2,1,0:T(4,128)(2,1)} copy(bf16[128,2,4,4,512]{4,0,3,2,1:T(8,128)(2,1)S(1)} %fusion.9) | data formatting | bytes 8388608 | tf_op jit(solution)/shard_map/convert_element_type | solution.py:115
  25.7 10.8 %all-to-all-start.2 = ((bf16[128,2,4,4,512]{4,3,2,1,0:T(4,128)(2,1)}), bf16[128,2,4,4,512]{4,3,2,1,0:T(4,128)(2,1)}, u32[]{:S(2)}, u32[]{:S(2)}) async-start(bf16[128,2,4,4,512]{4,3,2,1,0:T(4,128)(2,1)} %copy.54), calls=%async_computation.2 | async-start | bytes 8388608 | tf_op jit(solution)/shard_map/all_to_all | solution.py:116
  37.5 6.9 %fusion.8 = bf16[128,2,4,4,512]{4,0,3,2,1:T(8,128)(2,1)S(1)} fusion(bf16[4,1024,512]{2,1,0:T(8,128)(2,1)} %param.4, bf16[1,128,4,1024]{3,1,2,0:T(8,128)(2,1)S(1)} %copy.46, bf16[1,128,4,1024]{3,1,2,0:T(8,128)(2,1)S(1)} %copy.45), kind=kOutput, calls=%fused_computation.10 | convolution fusion | flops 4303355904 | bytes 10485760 | tf_op jit(solution)/shard_map/cdqp,rpk->dcqrk/dot_general | solution.py:114
  44.5 5.2 %copy.47 = bf16[128,2,4,4,512]{4,3,2,1,0:T(4,128)(2,1)} copy(bf16[128,2,4,4,512]{4,0,3,2,1:T(8,128)(2,1)S(1)} %fusion.8) | data formatting | bytes 8388608 | tf_op jit(solution)/shard_map/convert_element_type | solution.py:115
  49.6 39.5 %all-to-all-done.2 = bf16[128,2,4,4,512]{4,3,2,1,0:T(4,128)(2,1)} async-done(((bf16[128,2,4,4,512]{4,3,2,1,0:T(4,128)(2,1)}), bf16[128,2,4,4,512]{4,3,2,1,0:T(4,128)(2,1)}, u32[]{:S(2)}, u32[]{:S(2)}) %all-to-all-start.2) | async-done | bytes 4194336 | tf_op jit(solution)/shard_map/all_to_all | solution.py:116
  89.2 5.5 %all-to-all-start = ((bf16[128,2,4,4,512]{4,3,2,1,0:T(4,128)(2,1)}), bf16[128,2,4,4,512]{4,3,2,1,0:T(4,128)(2,1)}, u32[]{:S(2)}, u32[]{:S(2)}) async-start(bf16[128,2,4,4,512]{4,3,2,1,0:T(4,128)(2,1)} %copy.47), calls=%async_computation | async-start | bytes 8388608 | tf_op jit(solution)/shard_map/all_to_all | solution.py:116
  95.4 0.8 copy.58.refs_0_
  96.2 3.0 %copy.50 = bf16[256,32,32]{2,1,0:T(8,128)(2,1)S(1)} copy(bf16[256,32,32]{0,2,1:T(8,128)(2,1)S(1)} %copy-done) | data formatting | bytes 1048576 | tf_op args[2]
  99.2 11.2 %copy.82 = bf16[2,128,8,2048]{3,1,2,0:T(8,128)(2,1)} copy(bf16[2,128,8,2048]{3,2,1,0:T(8,128)(2,1)} %param.7) | data formatting | bytes 16777216 | tf_op args[3]
  110.9 0.7 reduce.5
  112.0 0.8 gather_fusion
  113.4 11.6 %reshape.483 = bf16[4,32,2,4,4,8,64]{6,5,4,3,2,1,0:T(8,128)(2,1)} reshape(bf16[128,2,4,4,512]{4,3,2,1,0:T(4,128)(2,1)} %all-to-all-done.2) | data formatting | bytes 8388608 | tf_op jit(solution)/shard_map/reshape | solution.py:117
  125.0 9.0 %fusion.5 = bf16[32,4,2,4,32,64]{5,4,3,2,1,0:T(8,128)(2,1)} fusion(bf16[32,4,32,4,8,1,1]{2,4,3,6,5,1,0:T(8,128)(2,1)S(1)} %bitcast.72, bf16[4,32,2,4,4,8,64]{6,5,4,3,2,1,0:T(8,128)(2,1)} %reshape.483), kind=kOutput, calls=%fused_computation.9 | convolution fusion | flops 136314880 | bytes 8650752 | tf_op jit(solution)/shard_map/jiasb,sjcqibx->jicqax/dot_general | solution.py:119
  134.0 12.3 %reshape.465.refs_2_ = bf16[1024,2048]{1,0:T(8,128)(2,1)} reshape(bf16[32,4,2,4,32,64]{5,4,3,2,1,0:T(8,128)(2,1)} %fusion.5) | data formatting | bytes 8388608 | tf_op jit(solution)/shard_map/reshape | solution.py:120
  146.3 1.2 all-to-all-done
  147.5 11.6 %reshape.481 = bf16[4,32,2,4,4,8,64]{6,5,4,3,2,1,0:T(8,128)(2,1)} reshape(bf16[128,2,4,4,512]{4,3,2,1,0:T(4,128)(2,1)} %all-to-all-done) | data formatting | bytes 8388608 | tf_op jit(solution)/shard_map/reshape | solution.py:117
  159.1 9.0 %fusion.2 = bf16[32,4,2,4,32,64]{5,4,3,2,1,0:T(8,128)(2,1)} fusion(bf16[32,4,32,4,8,1,1]{2,4,3,6,5,1,0:T(8,128)(2,1)S(1)} %bitcast.73, bf16[4,32,2,4,4,8,64]{6,5,4,3,2,1,0:T(8,128)(2,1)} %reshape.481), kind=kOutput, calls=%fused_computation.8 | convolution fusion | flops 136314880 | bytes 8650752 | tf_op jit(solution)/shard_map/jiasb,sjcqibx->jicqax/dot_general | solution.py:119
  168.1 12.4 %reshape.463.refs_1_ = bf16[1024,2048]{1,0:T(8,128)(2,1)} reshape(bf16[32,4,2,4,32,64]{5,4,3,2,1,0:T(8,128)(2,1)} %fusion.2) | data formatting | bytes 8388608 | tf_op jit(solution)/shard_map/reshape | solution.py:120
  180.5 25.3 %shard_map.46 = bf16[2,1024,2048]{2,1,0:T(8,128)(2,1)} custom-call(bf16[256,256]{1,0:T(8,128)(2,1)} %copy.58.refs_0_, bf16[1024,2048]{1,0:T(8,128)(2,1)} %reshape.463.refs_1_, bf16[1024,2048]{1,0:T(8,128)(2,1)} %reshape.465.refs_2_, bf16[2,8,128,2048]{3,2,1,0:T(8,128)(2,1)} %bitcast.71), custom_call_target="tpu_custom_call" | custom-call | tf_op jit(solution)/shard_map/pallas_call | solution.py:79
  (25 shorter events, 3.9 us)
Async XLA Ops:
  1.1 2.8 %copy-start.1 = (s32[4]{0:T(128)S(1)}, s32[4]{0:T(128)}, u32[]{:S(2)}) copy-start(s32[4]{0:T(128)} %param.5) | copy-start | bytes 52
  4.5 21.2 %all-to-all-start.1 = ((s32[32,1,4]{2,1,0:T(1,128)}), s32[32,1,4]{2,1,0:T(1,128)S(1)}, u32[]{:S(2)}, u32[]{:S(2)}) async-start(s32[32,1,4]{2,1,0:T(1,128)} %broadcast_in_dim.2), calls=%async_computation.1 | async-start | bytes 32768 | tf_op jit(solution)/shard_map/all_to_all | solution.py:111
  25.7 63.5 %all-to-all-start.2 = ((bf16[128,2,4,4,512]{4,3,2,1,0:T(4,128)(2,1)}), bf16[128,2,4,4,512]{4,3,2,1,0:T(4,128)(2,1)}, u32[]{:S(2)}, u32[]{:S(2)}) async-start(bf16[128,2,4,4,512]{4,3,2,1,0:T(4,128)(2,1)} %copy.54), calls=%async_computation.2 | async-start | bytes 8388608 | tf_op jit(solution)/shard_map/all_to_all | solution.py:116
  49.6 46.5 %copy-start = (bf16[256,32,32]{0,2,1:T(8,128)(2,1)S(1)}, bf16[256,32,32]{0,2,1:T(8,128)(2,1)}, u32[]{:S(2)}) copy-start(bf16[256,32,32]{0,2,1:T(8,128)(2,1)} %param.6) | copy-start | bytes 1572868
  89.2 58.3 %all-to-all-start = ((bf16[128,2,4,4,512]{4,3,2,1,0:T(4,128)(2,1)}), bf16[128,2,4,4,512]{4,3,2,1,0:T(4,128)(2,1)}, u32[]{:S(2)}, u32[]{:S(2)}) async-start(bf16[128,2,4,4,512]{4,3,2,1,0:T(4,128)(2,1)} %copy.47), calls=%async_computation | async-start | bytes 8388608 | tf_op jit(solution)/shard_map/all_to_all | solution.py:116
